TPU v7x, 256 devices: a whole 4x4x8 slice. The times are simulated.
256 devices in a mesh: frame: 16 (over z_hi, y), space: 16 (over z_lo, x, core).
Axes of the slice: x: 4, y: 4, z: 8 (z_hi: 4, z_lo: 2; z = z_hi * 2 + z_lo), core: 2. Of those that a mesh axis runs over, the one named last changes fastest.
Arguments:
- hidden_in: bfloat16 [2, 16, 32, 64, 1152], P(None, 'frame', 'space'), may hold values from -6 to 6
- attn_cotangent: bfloat16 [2, 16, 32, 64, 1152], P(None, 'frame', 'space'), may hold values from -6 to 6
- w_qkv: bfloat16 [1152, 3456], P('space'), may hold values from -0.1875 to 0.1875
- modulation_table: bfloat16 [1000, 2, 1152], replicated, may hold values from -3 to 3
- snr_table: float32 [1000], replicated, may hold values from 0.1 to 1
- timestep: int32 [2], replicated, may hold values from 0 to 999
- weight_index: int32 [2], replicated, may hold values from 0 to 999
Outputs:
- grad_input: bfloat16 [2, 16, 32, 64, 1152], P(None, 'frame', 'space')
- grad_w_qkv: float32 [1152, 3456], P('space')
- grad_modulation: float32 [2, 2, 1152], replicated
All inputs are finite; a program needn't handle non-finite values.
Results may differ from a plain program's by a relative error of at most 0.029.
Values may be sent and summed in bfloat16 or wider, within the bound.
A program may use at most 128 MiB of HBM per device.

v0:
```python
import jax
import jax.numpy as jnp
from jax import lax
from jax.sharding import PartitionSpec as P

HEADS = 16
HEAD_DIM = 72


def attend_back(queries, keys, values, upstream):
    factor = queries.shape[-1] ** (-0.5)
    queries = queries.astype(jnp.float32)
    keys = keys.astype(jnp.float32)
    values = values.astype(jnp.float32)
    upstream = upstream.astype(jnp.float32)
    highest = lax.Precision.HIGHEST
    scores = jnp.einsum("bfxhe,bgxhe->bxhfg", queries, keys, precision=highest) * factor
    expd = jnp.exp(scores)
    probs = expd / jnp.sum(expd, axis=-1, keepdims=True)
    grad_probs = jnp.einsum("bfxhe,bgxhe->bxhfg", upstream, values, precision=highest)
    grad_values = jnp.einsum("bxhfg,bfxhe->bgxhe", probs, upstream, precision=highest)
    grad_scores = probs * (grad_probs - jnp.sum(probs * grad_probs, axis=-1, keepdims=True))
    grad_queries = jnp.einsum("bxhfg,bgxhe->bfxhe", grad_scores, keys, precision=highest) * factor
    grad_keys = jnp.einsum("bxhfg,bfxhe->bgxhe", grad_scores, queries, precision=highest) * factor
    return (
        grad_queries.astype(jnp.bfloat16),
        grad_keys.astype(jnp.bfloat16),
        grad_values.astype(jnp.bfloat16),
    )


def per_device(
    hidden_in, attn_cotangent, w_qkv, modulation_table, snr_table, timestep, weight_index
):
    clip_count, frame_dev, row_dev, col_count, model_width = hidden_in.shape
    positions = row_dev * col_count
    values_in = hidden_in.astype(jnp.float32)
    average = jnp.mean(values_in, axis=-1, keepdims=True)
    centered = values_in - average
    variance = jnp.mean(centered * centered, axis=-1, keepdims=True)
    inverse_std = lax.rsqrt(variance + 1e-06)
    normed = centered * inverse_std
    modulation = modulation_table[timestep].astype(jnp.float32)
    shift = modulation[:, 0][:, None, None, None, :]
    scale = modulation[:, 1][:, None, None, None, :]
    modulated = (normed * (1.0 + scale) + shift).astype(jnp.bfloat16)
    mod_rows = modulated.reshape(-1, model_width)
    w_full = lax.all_gather(w_qkv, "space", axis=0, tiled=True)
    projected = jnp.dot(mod_rows, w_full, preferred_element_type=jnp.float32).astype(jnp.bfloat16)
    projected = projected.reshape(clip_count, frame_dev, positions, 3, model_width)
    loss_weight = snr_table[weight_index]
    upstream = (loss_weight[:, None, None, None, None] * attn_cotangent.astype(jnp.float32)).astype(
        jnp.bfloat16
    )
    upstream = upstream.reshape(clip_count, frame_dev, positions, 1, model_width)
    packed = jnp.concatenate([projected, upstream], axis=3)
    received = lax.all_to_all(packed, "frame", split_axis=2, concat_axis=1, tiled=True)
    item_count = received.shape[0]
    frames = received.shape[1]
    across = received.shape[2]
    pieces = received.reshape(item_count, frames, across, 4, HEADS, HEAD_DIM)
    head_grads = attend_back(
        pieces[:, :, :, 0], pieces[:, :, :, 1], pieces[:, :, :, 2], pieces[:, :, :, 3]
    )
    stacked = jnp.stack(head_grads, axis=3).reshape(item_count, frames, across, 3, model_width)
    grad_projected = lax.all_to_all(stacked, "frame", split_axis=1, concat_axis=2, tiled=True)
    grad_rows = grad_projected.reshape(-1, 3 * model_width)
    device_count = lax.axis_size("frame") * lax.axis_size("space")
    grad_scale_factor = float(mod_rows.shape[0] * device_count) ** (-0.5)
    row_share = lax.psum_scatter(
        lax.dot_general(
            mod_rows, grad_rows, (((0,), (0,)), ((), ())), preferred_element_type=jnp.float32
        ).astype(jnp.bfloat16),
        "space",
        scatter_dimension=0,
        tiled=True,
    )
    grad_weight = lax.psum(row_share, "frame").astype(jnp.float32) * grad_scale_factor
    grad_hidden = lax.dot_general(
        grad_rows, w_full, (((1,), (1,)), ((), ())), preferred_element_type=jnp.float32
    )
    grad_hidden = grad_hidden.reshape(values_in.shape)
    local_sums = jnp.stack(
        [jnp.sum(grad_hidden, axis=(1, 2, 3)), jnp.sum(grad_hidden * normed, axis=(1, 2, 3))],
        axis=1,
    )
    grad_modulation = lax.psum(local_sums, ("frame", "space")) * grad_scale_factor
    grad_normed = grad_hidden * (1.0 + scale)
    grad_input = (
        grad_normed
        - jnp.mean(grad_normed, axis=-1, keepdims=True)
        - normed * jnp.mean(grad_normed * normed, axis=-1, keepdims=True)
    ) * inverse_std
    return (grad_input.astype(jnp.bfloat16), grad_weight, grad_modulation)


def solution(mesh):
    in_specs = (
        P(None, "frame", "space", None, None),
        P(None, "frame", "space", None, None),
        P("space", None),
        P(),
        P(),
        P(),
        P(),
    )
    out_specs = (P(None, "frame", "space", None, None), P("space", None), P())
    return jax.shard_map(
        per_device, mesh=mesh, in_specs=in_specs, out_specs=out_specs, check_vma=False
    )
```

profile of v0, /device:TPU:2, one launch (start us, length us, event | category | flops | bytes accessed | tf_op | source)
XLA Modules:
  0.0 491.3 jit_solution(7075564899825200032)
XLA Ops:
  7.2 0.0 copy-start
  7.2 0.0 copy-start.2
  7.2 0.0 all-gather.2.cloned.1.call-start
  7.2 0.7 all-gather.2.cloned.1.call-update
  7.9 0.0 reduce-scatter.5.cloned.1.call-start
  8.0 0.7 compare_select_fusion.1
  8.6 2.9 gather_fusion
  11.6 0.7 compare_select_fusion
  12.3 0.0 copy-done
  12.3 0.6 gather_fusion.1
  12.9 1.2 multiply_convert_fusion.2
  14.2 0.6 copy.65
  14.8 0.0 copy-done.2
  14.8 0.2 convert_reduce_fusion
  15.0 0.0 copy-start.5
  15.0 0.3 fusion.18
  15.3 0.3 fusion.12
  15.6 0.0 copy-start.3
  15.6 49.8 %all-gather.2.cloned.1.call-done = bf16[1152,3456]{1,0:T(8,128)(2,1)} async-done(((bf16[72,3456]{1,0:T(8,128)(2,1)}), bf16[1152,3456]{1,0:T(8,128)(2,1)}) %all-gather.2.cloned.1.call-update) | async-done | bytes 7962640 | tf_op jit(solution)/shard_map/all_gather | solution.py:48
  65.4 0.0 copy-done.6
  65.4 0.0 copy-done.3
  65.5 7.1 %convolution_convert_fusion.1 = bf16[256,3456]{1,0:T(8,128)(2,1)} fusion(bf16[256,1152]{1,0:T(8,128)(2,1)S(1)} %bitcast.76, bf16[1152,3456]{1,0:T(8,128)(2,1)} %all-gather.2.cloned.1.call-done), kind=kOutput, calls=%fused_computation.3 | convolution fusion | flops 2039316480 | bytes 10321920 | tf_op jit(solution)/shard_map/dot_general | solution.py:49
  72.6 2.6 copy.63
  75.2 2.0 reshape.124
  77.2 4.6 pad_maximum_fusion
  81.8 4.9 copy.66
  86.7 67.7 %all_to_all.8 = bf16[2,1,128,4,1152]{4,3,1,0,2:T(4,128)(2,1)S(1)} all-to-all(bf16[2,1,128,4,1152]{4,3,1,0,2:T(4,128)(2,1)} %copy.66), channel_id=1, replica_groups=mesh['frame'=16,'space'=16] {'frame'}, dimensions={2} | all-to-all | bytes 4718592 | tf_op jit(solution)/shard_map/all_to_all | solution.py:57
  154.4 8.8 %reshape.148 = bf16[2,16,8,4,16,72]{5,4,3,0,2,1:T(8,128)(2,1)} reshape(bf16[2,1,128,4,1152]{4,3,1,0,2:T(4,128)(2,1)S(1)} %all_to_all.8) | data formatting | bytes 4718592 | tf_op jit(solution)/shard_map/reshape | solution.py:61
  163.2 3.6 fusion.25
  166.8 1.7 fusion.1
  168.5 1.8 multiply_reduce_fusion
  170.2 2.4 fusion.9
  172.7 2.2 fusion.10
  174.9 3.0 fusion.8
  177.9 0.3 copy.73
  178.2 1.5 stack.21
  179.7 0.3 copy.74
  180.0 1.3 stack.22
  181.4 1.5 copy.75
  182.9 1.3 stack.23
  184.2 0.2 pad_maximum_fusion.1
  184.4 0.1 copy.76
  184.6 40.6 %all_to_all.9 = bf16[2,16,8,3,1152]{4,2,0,3,1:T(8,128)(2,1)S(1)} all-to-all(bf16[2,16,8,3,1152]{4,2,0,3,1:T(8,128)(2,1)S(1)} %copy.76), channel_id=1, replica_groups=mesh['frame'=16,'space'=16] {'frame'}, dimensions={1} | all-to-all | bytes 3538944 | tf_op jit(solution)/shard_map/all_to_all | solution.py:66
  225.2 0.9 copy.77
  226.1 0.0 copy-start.4
  226.1 0.2 copy.90
  226.4 0.8 copy-done.4
  227.2 5.5 %convolution_convert_fusion = bf16[1152,3456]{1,0:T(8,128)(2,1)} fusion(bf16[256,1152]{1,0:T(8,128)(2,1)S(1)} %bitcast.77, bf16[256,3456]{1,0:T(8,128)(2,1)S(1)} %bitcast.73), kind=kOutput, calls=%fused_computation.2 | convolution fusion | flops 2042413056 | bytes 10321920 | tf_op jit(solution)/shard_map/dot_general | solution.py:71
  232.7 0.0 reduce-scatter.5.cloned.1.call-update
  232.7 0.0 all-reduce.3.cloned.1.call-start
  232.8 6.5 %fusion.19 = (f32[256]{0:T(256)}, f32[256,1152]{1,0:T(8,128)S(1)}) fusion(f32[2,1152]{1,0:T(2,128)S(1)} %bitcast.80, bf16[256,3456]{1,0:T(8,128)(2,1)S(1)} %bitcast.74, bf16[1152,3456]{1,0:T(8,128)(2,1)} %all-gather.2.cloned.1.call-done), kind=kOutput, calls=%fused_computation.34 | convolution fusion | flops 2039021312 | bytes 10921984 | tf_op jit(solution)/shard_map/dot_general | solution.py:79
  239.3 0.1 reduce_sum.78
  239.4 0.0 copy-done.5
  239.4 1.2 fusion.17
  240.6 77.9 %psum.15 = f32[2,2,1152]{2,0,1:T(2,128)S(1)} all-reduce(f32[2,2,1152]{2,0,1:T(2,128)S(1)} %pad_maximum_fusion.2), channel_id=1, replica_groups=mesh['frame'=16,'space'=16] {'frame','space'}, use_global_device_ids=true, to_apply=%region_10.0 | all-reduce | flops 4608 | bytes 36864 | tf_op jit(solution)/shard_map/psum | solution.py:87
  318.6 0.6 copy.80
  319.2 0.0 copy-done.8
  319.2 0.1 div.27
  319.3 0.0 all-reduce.3.cloned.1.call-update
  319.3 0.0 copy-done.7
  319.3 1.9 fusion.16
  321.2 161.5 %all-reduce.3.cloned.1.call-done = bf16[72,3456]{1,0:T(8,128)(2,1)} async-done(((bf16[72,3456]{1,0:T(8,128)(2,1)}), bf16[72,3456]{1,0:T(8,128)(2,1)}) %all-reduce.3.cloned.1.call-update) | async-done | bytes 497680 | tf_op jit(solution)/shard_map/psum | solution.py:78
  482.7 2.0 convert_multiply_fusion
  484.8 0.0 copy-done.1
  (18 shorter events, 0.1 us)
Async XLA Ops:
  7.2 5.1 %copy-start = (f32[1000]{0:T(1024)S(1)}, f32[1000]{0:T(1024)}, u32[]{:S(2)}) copy-start(f32[1000]{0:T(1024)} %param.11) | copy-start | bytes 12004
  7.2 7.6 %copy-start.2 = (bf16[2,1,2,64,1152]{4,3,2,1,0:T(8,128)(2,1)S(1)}, bf16[2,1,2,64,1152]{4,3,2,1,0:T(8,128)(2,1)}, u32[]{:S(2)}) copy-start(bf16[2,1,2,64,1152]{4,3,2,1,0:T(8,128)(2,1)} %param.7) | copy-start | bytes 1769476
  7.2 58.3 %all-gather.2.cloned.1.call-start = ((), (), s32[]{:S(2)}) async-start(), calls=%async_computation.3 | async-start | bytes 8460288 | tf_op jit(solution)/shard_map/all_gather | solution.py:48
  7.9 311.4 %reduce-scatter.5.cloned.1.call-start = ((), (), s32[]{:S(2)}) async-start(), calls=%async_computation.5 | async-start | bytes 8460288
  15.0 224.4 %copy-start.5 = (f32[2,2,64]{2,1,0:T(2,128)}, f32[2,2,64]{2,1,0:T(2,128)S(1)}, u32[]{:S(2)}) copy-start(f32[2,2,64]{2,1,0:T(2,128)S(1)} %broadcast_multiply_fusion.2) | copy-start | bytes 3076
  15.3 50.2 %copy-start.6 = (f32[2,2,64]{2,1,0:T(2,128)}, f32[2,2,64]{2,1,0:T(2,128)S(1)}, u32[]{:S(2)}) copy-start(f32[2,2,64]{2,1,0:T(2,128)S(1)} %add_rsqrt_fusion) | copy-start | bytes 3076
  15.6 49.8 %copy-start.3 = (bf16[2,1,2,64,1152]{4,3,2,1,0:T(8,128)(2,1)}, bf16[2,1,2,64,1152]{4,3,2,1,0:T(8,128)(2,1)S(1)}, u32[]{:S(2)}) copy-start(bf16[2,1,2,64,1152]{4,3,2,1,0:T(8,128)(2,1)S(1)} %fusion.12) | copy-start | bytes 1769476
  226.1 1.1 copy-start.4
  232.7 250.0 %all-reduce.3.cloned.1.call-start = ((), (), s32[]{:S(2)}) async-start(), calls=%async_computation.4 | async-start | bytes 995328 | tf_op jit(solution)/shard_map/psum | solution.py:78
  239.3 79.9 %copy-start.8 = (f32[256]{0:T(256)S(1)}, f32[256]{0:T(256)}, u32[]{:S(2)}) copy-start(f32[256]{0:T(256)} %get-tuple-element.25) | copy-start | bytes 3076
  239.4 79.9 %copy-start.7 = (f32[2,2,64]{2,1,0:T(2,128)S(1)}, f32[2,2,64]{2,1,0:T(2,128)}, u32[]{:S(2)}) copy-start(f32[2,2,64]{2,1,0:T(2,128)} %copy-done.6) | copy-start | bytes 3076
  319.3 165.5 %copy-start.1 = (f32[1000]{0:T(1024)S(1)}, f32[1000]{0:T(1024)}, u32[]{:S(2)}) copy-start(f32[1000]{0:T(1024)} %param.11) | copy-start | bytes 12004
Sparse Core Ops, SparseCore 0:
  9.9 55.5 all-gather.1
  232.9 74.6 reduce-scatter.4
  319.4 163.2 all-reduce.2
where the time goes:
time: 492 us; the launch traced here: 491 us
  waiting for transfers between devices  212 us (43%)
  blocking collectives  186 us (38%)
  local copies, waits for them, and re-layouts  35.1 us (7%)
  matrix products  30.3 us (6%)
  between operations  14 us (3%)
  other arithmetic  13.4 us (3%)
    psum x1, waiting for transfers between devices, per_device(): lax.psum(row_share, 'frame').astype(jnp.float32) * grad_scale_factor  162 us
    psum x1, blocking collectives, per_device(): lax.psum(local_sums, ('frame', 'space')) * grad_scale_factor  77.9 us
    all_to_all x1, blocking collectives, per_device(): lax.all_to_all(packed, 'frame', split_axis=2, concat_axis=1, tiled=True)  67.7 us
    all_gather x1, waiting for transfers between devices, per_device(): w_full = lax.all_gather(w_qkv, 'space', axis=0, tiled=True)  49.8 us
    all_to_all x1, blocking collectives, per_device(): lax.all_to_all(stacked, 'frame', split_axis=1, concat_axis=2, tiled=True)  40.6 us
  transfers between devices with their start and end apart: 3, of which 2 were waited for; matrix products, arithmetic and copies ran while one was open for 4% of the time, Pallas kernels for 0%

commit v1 on v0

--- a/solution.py
+++ b/solution.py
@@ -5,6 +5,11 @@
 
 HEADS = 16
 HEAD_DIM = 72
+
+
+def by_each_axis(value, inner_axis, outer_axis):
+    inner = lax.psum(value, inner_axis)
+    return lax.psum(inner, outer_axis)
 
 
 def attend_back(queries, keys, values, upstream):
@@ -84,7 +89,7 @@
         [jnp.sum(grad_hidden, axis=(1, 2, 3)), jnp.sum(grad_hidden * normed, axis=(1, 2, 3))],
         axis=1,
     )
-    grad_modulation = lax.psum(local_sums, ("frame", "space")) * grad_scale_factor
+    grad_modulation = by_each_axis(local_sums, "frame", "space") * grad_scale_factor
     grad_normed = grad_hidden * (1.0 + scale)
     grad_input = (
         grad_normed

time: 492 us -> 545 us (1.11)
  blocking collectives: 186 us -> 239 us
    psum x1 -> x2, blocking collectives: 77.9 us -> 131 us  [the longest x1 81.5 us: by_each_axis(): inner = lax.psum(value, inner_axis)]
  transfers between devices with their start and end apart: 3 -> 3, of which waited for: 2 -> 2; matrix products, arithmetic and copies ran while one was open for 4% -> 3% of each run, Pallas kernels for 0% -> 0%
where the time goes in v1:
time: 545 us; the launch traced here: 544 us
  blocking collectives  239 us (44%)
  waiting for transfers between devices  212 us (39%)
  local copies, waits for them, and re-layouts  35.1 us (6%)
  matrix products  30.3 us (6%)
  between operations  14 us (3%)
  other arithmetic  13.4 us (2%)
    psum x1, waiting for transfers between devices, per_device(): lax.psum(row_share, 'frame').astype(jnp.float32) * grad_scale_factor  161 us
    psum x1, blocking collectives, by_each_axis(): inner = lax.psum(value, inner_axis)  81.5 us
    all_to_all x1, blocking collectives, per_device(): lax.all_to_all(packed, 'frame', split_axis=2, concat_axis=1, tiled=True)  67.7 us
    all_gather x1, waiting for transfers between devices, per_device(): w_full = lax.all_gather(w_qkv, 'space', axis=0, tiled=True)  49.8 us
    psum x1, blocking collectives, by_each_axis(): return lax.psum(inner, outer_axis)  49.6 us
    all_to_all x1, blocking collectives, per_device(): lax.all_to_all(stacked, 'frame', split_axis=1, concat_axis=2, tiled=True)  40.6 us
  transfers between devices with their start and end apart: 3, of which 2 were waited for; matrix products, arithmetic and copies ran while one was open for 3% of the time, Pallas kernels for 0%

profile of v1, /device:TPU:2, one launch (start us, length us, event | category | flops | bytes accessed | tf_op | source)
XLA Modules:
  0.0 544.2 jit_solution(5557345247216517840)
XLA Ops:
  7.2 0.0 copy-start
  7.2 0.0 copy-start.2
  7.2 0.0 all-gather.2.cloned.1.call-start
  7.2 0.7 all-gather.2.cloned.1.call-update
  7.9 0.0 reduce-scatter.5.cloned.1.call-start
  8.0 0.7 compare_select_fusion.1
  8.6 2.9 gather_fusion
  11.6 0.7 compare_select_fusion
  12.3 0.0 copy-done
  12.3 0.6 gather_fusion.1
  12.9 1.2 multiply_convert_fusion.2
  14.2 0.6 copy.65
  14.8 0.0 copy-done.2
  14.8 0.2 convert_reduce_fusion
  15.0 0.0 copy-start.5
  15.0 0.3 fusion.18
  15.3 0.3 fusion.12
  15.6 0.0 copy-start.3
  15.6 49.8 %all-gather.2.cloned.1.call-done = bf16[1152,3456]{1,0:T(8,128)(2,1)} async-done(((bf16[72,3456]{1,0:T(8,128)(2,1)}), bf16[1152,3456]{1,0:T(8,128)(2,1)}) %all-gather.2.cloned.1.call-update) | async-done | bytes 7962640 | tf_op jit(solution)/shard_map/all_gather | solution.py:53
  65.4 0.0 copy-done.6
  65.4 0.0 copy-done.3
  65.5 7.1 %convolution_convert_fusion.1 = bf16[256,3456]{1,0:T(8,128)(2,1)} fusion(bf16[256,1152]{1,0:T(8,128)(2,1)S(1)} %bitcast.76, bf16[1152,3456]{1,0:T(8,128)(2,1)} %all-gather.2.cloned.1.call-done), kind=kOutput, calls=%fused_computation.3 | convolution fusion | flops 2039316480 | bytes 10321920 | tf_op jit(solution)/shard_map/dot_general | solution.py:54
  72.6 2.6 copy.63
  75.2 2.0 reshape.124
  77.2 4.6 pad_maximum_fusion
  81.8 4.9 copy.66
  86.7 67.7 %all_to_all.8 = bf16[2,1,128,4,1152]{4,3,1,0,2:T(4,128)(2,1)S(1)} all-to-all(bf16[2,1,128,4,1152]{4,3,1,0,2:T(4,128)(2,1)} %copy.66), channel_id=1, replica_groups=mesh['frame'=16,'space'=16] {'frame'}, dimensions={2} | all-to-all | bytes 4718592 | tf_op jit(solution)/shard_map/all_to_all | solution.py:62
  154.4 8.8 %reshape.148 = bf16[2,16,8,4,16,72]{5,4,3,0,2,1:T(8,128)(2,1)} reshape(bf16[2,1,128,4,1152]{4,3,1,0,2:T(4,128)(2,1)S(1)} %all_to_all.8) | data formatting | bytes 4718592 | tf_op jit(solution)/shard_map/reshape | solution.py:66
  163.2 3.6 fusion.25
  166.8 1.7 fusion.1
  168.5 1.8 multiply_reduce_fusion
  170.2 2.4 fusion.9
  172.7 2.2 fusion.10
  174.9 3.0 fusion.8
  177.9 0.3 copy.73
  178.2 1.5 stack.21
  179.7 0.3 copy.74
  180.0 1.3 stack.22
  181.4 1.5 copy.75
  182.9 1.3 stack.23
  184.2 0.2 pad_maximum_fusion.1
  184.4 0.1 copy.76
  184.6 40.6 %all_to_all.9 = bf16[2,16,8,3,1152]{4,2,0,3,1:T(8,128)(2,1)S(1)} all-to-all(bf16[2,16,8,3,1152]{4,2,0,3,1:T(8,128)(2,1)S(1)} %copy.76), channel_id=1, replica_groups=mesh['frame'=16,'space'=16] {'frame'}, dimensions={1} | all-to-all | bytes 3538944 | tf_op jit(solution)/shard_map/all_to_all | solution.py:71
  225.2 0.9 copy.77
  226.1 0.0 copy-start.4
  226.1 0.2 copy.90
  226.4 0.8 copy-done.4
  227.2 5.5 %convolution_convert_fusion = bf16[1152,3456]{1,0:T(8,128)(2,1)} fusion(bf16[256,1152]{1,0:T(8,128)(2,1)S(1)} %bitcast.77, bf16[256,3456]{1,0:T(8,128)(2,1)S(1)} %bitcast.73), kind=kOutput, calls=%fused_computation.2 | convolution fusion | flops 2042413056 | bytes 10321920 | tf_op jit(solution)/shard_map/dot_general | solution.py:76
  232.7 0.0 reduce-scatter.5.cloned.1.call-update
  232.7 0.0 all-reduce.3.cloned.1.call-start
  232.8 6.5 %fusion.19 = (f32[256]{0:T(256)}, f32[256,1152]{1,0:T(8,128)S(1)}) fusion(f32[2,1152]{1,0:T(2,128)S(1)} %bitcast.80, bf16[256,3456]{1,0:T(8,128)(2,1)S(1)} %bitcast.74, bf16[1152,3456]{1,0:T(8,128)(2,1)} %all-gather.2.cloned.1.call-done), kind=kOutput, calls=%fused_computation.34 | convolution fusion | flops 2039021312 | bytes 10921984 | tf_op jit(solution)/shard_map/dot_general | solution.py:84
  239.3 0.1 reduce_sum.78
  239.4 0.0 copy-done.5
  239.4 1.2 fusion.17
  240.6 81.5 %psum.22 = f32[2,2,1152]{2,0,1:T(2,128)S(1)} all-reduce(f32[2,2,1152]{2,0,1:T(2,128)S(1)} %pad_maximum_fusion.2), channel_id=1, replica_groups=mesh['frame'=16,'space'=16] {'frame'}, use_global_device_ids=true, to_apply=%region_10.0 | all-reduce | flops 4608 | bytes 36864 | tf_op jit(solution)/shard_map/psum | solution.py:11
  322.1 49.6 %psum.23 = f32[2,2,1152]{2,0,1:T(2,128)S(1)} all-reduce(f32[2,2,1152]{2,0,1:T(2,128)S(1)} %psum.22), channel_id=1, replica_groups=mesh['frame'=16,'space'=16] {'space'}, use_global_device_ids=true, to_apply=%region_11.0 | all-reduce | flops 4608 | bytes 36864 | tf_op jit(solution)/shard_map/psum | solution.py:12
  371.7 0.6 copy.80
  372.3 0.0 copy-done.8
  372.3 0.1 div.27
  372.4 0.0 all-reduce.3.cloned.1.call-update
  372.5 0.0 copy-done.7
  372.5 1.9 fusion.16
  374.4 161.3 %all-reduce.3.cloned.1.call-done = bf16[72,3456]{1,0:T(8,128)(2,1)} async-done(((bf16[72,3456]{1,0:T(8,128)(2,1)}), bf16[72,3456]{1,0:T(8,128)(2,1)}) %all-reduce.3.cloned.1.call-update) | async-done | bytes 497680 | tf_op jit(solution)/shard_map/psum | solution.py:83
  535.6 2.0 convert_multiply_fusion
  (19 shorter events, 0.1 us)
Async XLA Ops:
  7.2 5.1 copy-start
  7.2 7.6 %copy-start.2 = (bf16[2,1,2,64,1152]{4,3,2,1,0:T(8,128)(2,1)S(1)}, bf16[2,1,2,64,1152]{4,3,2,1,0:T(8,128)(2,1)}, u32[]{:S(2)}) copy-start(bf16[2,1,2,64,1152]{4,3,2,1,0:T(8,128)(2,1)} %param.7) | copy-start | bytes 1769476
  7.2 58.3 %all-gather.2.cloned.1.call-start = ((), (), s32[]{:S(2)}) async-start(), calls=%async_computation.3 | async-start | bytes 8460288 | tf_op jit(solution)/shard_map/all_gather | solution.py:53
  7.9 364.5 %reduce-scatter.5.cloned.1.call-start = ((), (), s32[]{:S(2)}) async-start(), calls=%async_computation.5 | async-start | bytes 8460288
  15.0 224.4 %copy-start.5 = (f32[2,2,64]{2,1,0:T(2,128)}, f32[2,2,64]{2,1,0:T(2,128)S(1)}, u32[]{:S(2)}) copy-start(f32[2,2,64]{2,1,0:T(2,128)S(1)} %broadcast_multiply_fusion.2) | copy-start | bytes 3076
  15.3 50.2 %copy-start.6 = (f32[2,2,64]{2,1,0:T(2,128)}, f32[2,2,64]{2,1,0:T(2,128)S(1)}, u32[]{:S(2)}) copy-start(f32[2,2,64]{2,1,0:T(2,128)S(1)} %add_rsqrt_fusion) | copy-start | bytes 3076
  15.6 49.8 %copy-start.3 = (bf16[2,1,2,64,1152]{4,3,2,1,0:T(8,128)(2,1)}, bf16[2,1,2,64,1152]{4,3,2,1,0:T(8,128)(2,1)S(1)}, u32[]{:S(2)}) copy-start(bf16[2,1,2,64,1152]{4,3,2,1,0:T(8,128)(2,1)S(1)} %fusion.12) | copy-start | bytes 1769476
  226.1 1.1 copy-start.4
  232.7 302.9 %all-reduce.3.cloned.1.call-start = ((), (), s32[]{:S(2)}) async-start(), calls=%async_computation.4 | async-start | bytes 995328 | tf_op jit(solution)/shard_map/psum | solution.py:83
  239.3 133.1 %copy-start.8 = (f32[256]{0:T(256)S(1)}, f32[256]{0:T(256)}, u32[]{:S(2)}) copy-start(f32[256]{0:T(256)} %get-tuple-element.25) | copy-start | bytes 3076
  239.4 133.1 %copy-start.7 = (f32[2,2,64]{2,1,0:T(2,128)S(1)}, f32[2,2,64]{2,1,0:T(2,128)}, u32[]{:S(2)}) copy-start(f32[2,2,64]{2,1,0:T(2,128)} %copy-done.6) | copy-start | bytes 3076
  372.4 165.2 %copy-start.1 = (f32[1000]{0:T(1024)S(1)}, f32[1000]{0:T(1024)}, u32[]{:S(2)}) copy-start(f32[1000]{0:T(1024)} %param.11) | copy-start | bytes 12004
Sparse Core Ops, SparseCore 0:
  9.9 55.5 all-gather.1
  232.9 75.3 reduce-scatter.4
  372.6 162.9 all-reduce.2
